TPU v7x, 32 devices: a whole 2x2x4 slice. The times are simulated.
32 devices in a mesh: replica: 4 (over y, core), dp: 8 (over z, x).
Axes of the slice: x: 2, y: 2, z: 4, core: 2. Of those that a mesh axis runs over, the one named last changes fastest.
Arguments:
- features: bfloat16 [3072, 256], P('dp'), may hold values from -160 to 160
- prototypes: bfloat16 [256, 131072], P(None, ('replica', 'dp')), may hold values from -120 to 120
Outputs:
- codes: bfloat16 [3072, 131072], P('dp', 'replica')
All inputs are finite; a program needn't handle non-finite values.
Results may differ from a plain program's by a relative error of at most 0.0058.
Values may be sent and summed in bfloat16 or wider, within the bound.
No kernel may reach another device: no remote copies, remote signals or barrier semaphores. Data moves between devices by JAX's collectives and lax.ppermute only.
A program may use at most 192 MiB of HBM per device.

v0:
```python
import jax
import jax.numpy as jnp
from jax import lax
from jax.sharding import PartitionSpec as P

PROTOS = 131072
ITERS = 3


epsilon = 1e-06
sharpness_divisor = 0.07


def unit_rows(values):
    return values * lax.rsqrt(jnp.sum(values * values, axis=1, keepdims=True) + epsilon)


def unit_columns(values):
    return values * lax.rsqrt(jnp.sum(values * values, axis=0, keepdims=True) + epsilon)


def scaled_codes(kernel_entries, row_scale_factors, cols_scale):
    return (
        PROTOS
        * kernel_entries.astype(jnp.float32)
        * row_scale_factors[:, None]
        * cols_scale[None, :]
    ).astype(jnp.bfloat16)


def local(features, prototypes):
    normalised_embeddings = unit_rows(features.astype(jnp.float32)).astype(jnp.bfloat16)
    tempered_scores = unit_columns(
        lax.all_gather(prototypes, "dp", axis=1, tiled=True).astype(jnp.float32)
    ).astype(jnp.bfloat16)
    scores = jnp.dot(normalised_embeddings, tempered_scores, preferred_element_type=jnp.float32)
    kernel_entries = jnp.exp(scores / sharpness_divisor).astype(jnp.bfloat16)
    row_scale_factors = jnp.ones((kernel_entries.shape[0],), jnp.float32)
    cols_scale = jnp.ones((kernel_entries.shape[1],), jnp.float32)
    for iteration in range(ITERS):
        incomplete_column_totals = jnp.dot(
            row_scale_factors.astype(jnp.bfloat16),
            kernel_entries,
            preferred_element_type=jnp.float32,
        )
        cols_scale = 1.0 / lax.psum(incomplete_column_totals, "dp")
        partial_rows = jnp.dot(
            kernel_entries, cols_scale.astype(jnp.bfloat16), preferred_element_type=jnp.float32
        )
        row_scale_factors = 1.0 / lax.psum(partial_rows, "replica")
    return scaled_codes(kernel_entries, row_scale_factors, cols_scale)


def solution(mesh):
    placed = (P("dp", None), P(None, ("replica", "dp")))
    return jax.shard_map(
        local, mesh=mesh, in_specs=placed, out_specs=P("dp", "replica"), check_vma=False
    )
```

profile of v0, /device:TPU:0, one launch (start us, length us, event | category | flops | bytes accessed | tf_op | source)
XLA Modules:
  0.0 596.2 jit_solution(7549559591904931822)
XLA Ops:
  6.5 0.0 all-gather.2.cloned.1.call-start
  6.5 0.7 all-gather.2.cloned.1.call-update
  7.3 0.0 all-reduce.4.cloned.1.call-start
  7.3 1.1 fusion.4
  8.4 231.1 %all-gather.2.cloned.1.call-done = bf16[256,32768]{1,0:T(8,128)(2,1)} async-done(((bf16[256,4096]{1,0:T(8,128)(2,1)}), bf16[256,32768]{1,0:T(8,128)(2,1)}) %all-gather.2.cloned.1.call-update) | async-done | bytes 16777232 | tf_op jit(solution)/shard_map/all_gather | solution.py:34
  239.5 7.1 %fusion = f32[32768]{0:T(1024)S(1)} fusion(bf16[256,32768]{1,0:T(8,128)(2,1)} %all-gather.2.cloned.1.call-done), kind=kLoop, calls=%fused_computation.4 | loop fusion | flops 25133056 | bytes 16908288 | tf_op jit(solution)/shard_map/reduce_sum | solution.py:19
  246.7 19.9 %exponential_convert_fusion = bf16[384,32768]{1,0:T(8,128)(2,1)} fusion(bf16[256,32768]{1,0:T(8,128)(2,1)} %all-gather.2.cloned.1.call-done, f32[32768]{0:T(1024)S(1)} %add_rsqrt_fusion, bf16[384,256]{1,0:T(8,128)(2,1)} %param.2, f32[384]{0:T(512)S(1)} %add_rsqrt_fusion.1), kind=kOutput, calls=%fused_computation.1 | convolution fusion | flops 6493077504 | bytes 42272256 | tf_op jit(solution)/shard_map/dot_general | solution.py:36
  266.5 12.2 %fusion.8 = f32[1,32768]{1,0:T(1,128)} fusion(bf16[384,32768]{1,0:T(8,128)(2,1)} %exponential_convert_fusion), kind=kOutput, calls=%fused_computation.23 | convolution fusion | flops 25165824 | bytes 25296896 | tf_op jit(solution)/shard_map/dot_general | solution.py:41
  278.7 0.0 all-reduce.4.cloned.1.call-update
  278.7 0.0 all-reduce.6.cloned.1.call-start
  278.8 68.8 %all-reduce.4.cloned.1.call-done = f32[32768]{0:T(1024)} async-done(((f32[32768]{0:T(1024)}), f32[32768]{0:T(1024)}) %all-reduce.4.cloned.1.call-update) | async-done | bytes 131088 | tf_op jit(solution)/shard_map/psum | solution.py:46
  347.6 0.9 divide_convert_fusion.1
  348.5 0.1 reshape.16
  348.6 11.5 %convolution_reduce_fusion.2 = f32[384]{0:T(512)S(1)} fusion(bf16[384,32768]{1,0:T(8,128)(2,1)} %exponential_convert_fusion, bf16[32768,1]{0,1:T(2,128)(2,1)S(1)} %reshape.16), kind=kOutput, calls=%fused_computation.9 | convolution fusion | flops 25165824 | bytes 25232896 | tf_op jit(solution)/shard_map/dot_general | solution.py:47
  360.1 5.8 psum.43
  366.0 12.2 %fusion.12 = f32[1,32768]{1,0:T(1,128)} fusion(bf16[384,1]{0,1:T(2,128)(2,1)S(1)} %reshape.18, bf16[384,32768]{1,0:T(8,128)(2,1)} %exponential_convert_fusion), kind=kOutput, calls=%fused_computation.27 | convolution fusion | flops 25165824 | bytes 25297664 | tf_op jit(solution)/shard_map/dot_general | solution.py:41
  378.1 0.0 all-reduce.6.cloned.1.call-update
  378.2 0.0 all-reduce.8.cloned.1.call-start
  378.2 69.9 %all-reduce.6.cloned.1.call-done = f32[32768]{0:T(1024)} async-done(((f32[32768]{0:T(1024)}), f32[32768]{0:T(1024)}) %all-reduce.6.cloned.1.call-update) | async-done | bytes 131088 | tf_op jit(solution)/shard_map/psum | solution.py:46
  448.2 0.9 divide_convert_fusion
  449.1 0.1 reshape.20
  449.2 11.5 %convolution_reduce_fusion.1 = f32[384]{0:T(512)S(1)} fusion(bf16[384,32768]{1,0:T(8,128)(2,1)} %exponential_convert_fusion, bf16[32768,1]{0,1:T(2,128)(2,1)S(1)} %reshape.20), kind=kOutput, calls=%fused_computation.8 | convolution fusion | flops 25165824 | bytes 25232896 | tf_op jit(solution)/shard_map/dot_general | solution.py:47
  460.7 5.9 psum.45
  466.6 12.2 %fusion.13 = f32[1,32768]{1,0:T(1,128)} fusion(bf16[384,1]{0,1:T(2,128)(2,1)S(1)} %reshape.22, bf16[384,32768]{1,0:T(8,128)(2,1)} %exponential_convert_fusion), kind=kOutput, calls=%fused_computation.28 | convolution fusion | flops 25165824 | bytes 25297664 | tf_op jit(solution)/shard_map/dot_general | solution.py:41
  478.8 0.0 all-reduce.8.cloned.1.call-update
  478.8 70.0 %all-reduce.8.cloned.1.call-done = f32[32768]{0:T(1024)} async-done(((f32[32768]{0:T(1024)}), f32[32768]{0:T(1024)}) %all-reduce.8.cloned.1.call-update) | async-done | bytes 131088 | tf_op jit(solution)/shard_map/psum | solution.py:46
  548.8 0.9 fusion.11
  549.7 0.1 reshape.24
  549.8 11.5 %convolution_reduce_fusion = f32[384]{0:T(512)S(1)} fusion(bf16[384,32768]{1,0:T(8,128)(2,1)} %exponential_convert_fusion, bf16[32768,1]{0,1:T(2,128)(2,1)S(1)} %reshape.24), kind=kOutput, calls=%fused_computation.7 | convolution fusion | flops 25165824 | bytes 25232896 | tf_op jit(solution)/shard_map/dot_general | solution.py:47
  561.4 5.7 psum.47
  567.0 22.7 %multiply_convert_fusion = bf16[384,32768]{1,0:T(8,128)(2,1)} fusion(bf16[384,32768]{1,0:T(8,128)(2,1)} %exponential_convert_fusion, f32[32768]{0:T(1024)S(1)} %get-tuple-element.6, f32[384]{0:T(512)S(1)} %divide_multiply_fusion), kind=kLoop, calls=%fused_computation | loop fusion | flops 50331648 | bytes 50464256 | tf_op jit(solution)/shard_map/convert_element_type | solution.py:28
  (7 shorter events, 0.1 us)
Async XLA Ops:
  6.5 233.0 %all-gather.2.cloned.1.call-start = ((), (), s32[]{:S(2)}) async-start(), calls=%async_computation | async-start | bytes 18874368 | tf_op jit(solution)/shard_map/all_gather | solution.py:34
  7.3 340.3 %all-reduce.4.cloned.1.call-start = ((), (), s32[]{:S(2)}) async-start(), calls=%async_computation.1 | async-start | bytes 262144 | tf_op jit(solution)/shard_map/psum | solution.py:46
  278.7 169.4 %all-reduce.6.cloned.1.call-start = ((), (), s32[]{:S(2)}) async-start(), calls=%async_computation.2 | async-start | bytes 262144 | tf_op jit(solution)/shard_map/psum | solution.py:46
  378.2 170.6 %all-reduce.8.cloned.1.call-start = ((), (), s32[]{:S(2)}) async-start(), calls=%async_computation.3 | async-start | bytes 262144 | tf_op jit(solution)/shard_map/psum | solution.py:46
Sparse Core Ops, SparseCore 0:
  9.5 229.9 all-gather.1
  278.9 68.6 all-reduce.3
  378.3 69.8 all-reduce.5
  478.9 69.8 all-reduce.7
where the time goes:
time: 597 us; the launch traced here: 596 us
  waiting for transfers between devices  441 us (74%)
  matrix products  91 us (15%)
  other arithmetic  33.7 us (6%)
  blocking collectives  17.4 us (3%)
  between operations  13.2 us (2%)
    all_gather x1, waiting for transfers between devices, local(): lax.all_gather(prototypes, 'dp', axis=1, tiled=True).astype(jnp.float32)  231 us
    psum x3, waiting for transfers between devices, local(): cols_scale = 1.0 / lax.psum(incomplete_column_totals, 'dp')  209 us
    dot_general x3, matrix products, local(): jnp.dot(row_scale_factors.astype(jnp.bfloat16), kernel_entries, preferred...  36.5 us
    dot_general x3, matrix products, local(): jnp.dot(kernel_entries, cols_scale.astype(jnp.bfloat16), preferred_elemen...  34.6 us
    convert_element_type x1, other arithmetic, scaled_codes(): return (PROTOS * kernel_entries.astype(jnp.float32) * row_scale_factors[:...  22.7 us
    dot_general x1, matrix products, local(): jnp.dot(normalised_embeddings, tempered_scores, preferred_element_type=jn...  19.9 us
    psum x3, blocking collectives, local(): row_scale_factors = 1.0 / lax.psum(partial_rows, 'replica')  17.4 us
  transfers between devices with their start and end apart: 4, of which 4 were waited for; matrix products, arithmetic and copies ran while one was open for 0% of the time, Pallas kernels for 0%

commit v1 on v0

v1 whole, which is shorter than its diff:
```python
import jax
import jax.numpy as jnp
from jax import lax
from jax.sharding import PartitionSpec as P

PROTOS = 131072
ITERS = 3


epsilon = 1e-06
sharpness_divisor = 0.07


def unit_rows(values):
    return values * lax.rsqrt(jnp.sum(values * values, axis=1, keepdims=True) + epsilon)


def unit_columns(values):
    return values * lax.rsqrt(jnp.sum(values * values, axis=0, keepdims=True) + epsilon)


def kernel_of(features, prototypes):
    normed = unit_rows(features.astype(jnp.float32)).astype(jnp.bfloat16)
    unit = unit_columns(prototypes.astype(jnp.float32)).astype(jnp.bfloat16)
    scores = jnp.dot(normed, unit, preferred_element_type=jnp.float32)
    return jnp.exp(scores / sharpness_divisor).astype(jnp.bfloat16)


def local(features, prototypes):
    rows = features.shape[0]
    mine = kernel_of(lax.all_gather(features, "dp", axis=0, tiled=True), prototypes)
    row_scale = jnp.ones((mine.shape[0],), jnp.float32)
    for _ in range(ITERS):
        col_scale = 1.0 / jnp.dot(row_scale.astype(jnp.bfloat16), mine, preferred_element_type=jnp.float32)
        partial = jnp.dot(mine, col_scale.astype(jnp.bfloat16), preferred_element_type=jnp.float32)
        row_scale = 1.0 / lax.psum(partial, ("dp", "replica"))
    col_scale = lax.all_gather(col_scale, "dp", axis=0, tiled=True)
    row_scale = lax.dynamic_slice_in_dim(row_scale, lax.axis_index("dp") * rows, rows)
    entries = kernel_of(features, lax.all_gather(prototypes, "dp", axis=1, tiled=True))
    return (
        PROTOS * entries.astype(jnp.float32) * row_scale[:, None] * col_scale[None, :]
    ).astype(jnp.bfloat16)


def solution(mesh):
    placed = (P("dp", None), P(None, ("replica", "dp")))
    return jax.shard_map(
        local, mesh=mesh, in_specs=placed, out_specs=P("dp", "replica"), check_vma=False
    )
```

time: 597 us -> 354 us (0.59)
  waiting for transfers between devices: 441 us -> 46.7 us
  blocking collectives: 17.4 us -> 173 us
  other arithmetic: 33.7 us -> 12.3 us
  matrix products: 91 us -> 104 us
    psum x3 -> x0, waiting for transfers between devices: 209 us -> none  [local(): cols_scale = 1.0 / lax.psum(incomplete_column_totals, 'dp')]
    all_gather x1 -> x2, waiting for transfers between devices: 231 us -> 45.3 us  [the longest x1 45.3 us: local(): lax.all_gather(features, 'dp', axis=0, tiled=True)]
    psum x3, blocking collectives: 17.4 us -> 140 us  [local(): row_scale = 1.0 / lax.psum(partial, ('dp', 'replica'))]
    all_gather x0 -> x1, blocking collectives: none -> 32.1 us  [local(): col_scale = lax.all_gather(col_scale, 'dp', axis=0, tiled=True)]
    convert_element_type x6 -> x5, other arithmetic: 25.5 us -> 0.04 us  [the longest x3 0.02 us: local(): col_scale.astype(jnp.bfloat16)]
    dot_general x7 -> x8, matrix products: 91 us -> 104 us  [the longest x2 40.9 us: kernel_of(): scores = jnp.dot(normed, unit, preferred_element_type=jnp.float32)]
  transfers between devices with their start and end apart: 4 -> 2, of which waited for: 4 -> 1; matrix products, arithmetic and copies ran while one was open for 0% -> 24% of each run, Pallas kernels for 0% -> 0%
where the time goes in v1:
time: 354 us; the launch traced here: 353 us
  blocking collectives  173 us (49%)
  matrix products  104 us (29%)
  waiting for transfers between devices  46.7 us (13%)
  between operations  13.5 us (4%)
  other arithmetic  12.3 us (3%)
  local copies, waits for them, and re-layouts  4.04 us (1%)
    psum x3, blocking collectives, local(): row_scale = 1.0 / lax.psum(partial, ('dp', 'replica'))  140 us
    all_gather x1, waiting for transfers between devices, local(): lax.all_gather(features, 'dp', axis=0, tiled=True)  45.3 us
    dot_general x2, matrix products, kernel_of(): scores = jnp.dot(normed, unit, preferred_element_type=jnp.float32)  40.9 us
    dot_general x3, matrix products, local(): jnp.dot(row_scale.astype(jnp.bfloat16), mine, preferred_element_type=jnp....  33.5 us
    all_gather x1, blocking collectives, local(): col_scale = lax.all_gather(col_scale, 'dp', axis=0, tiled=True)  32.1 us
    dot_general x3, matrix products, local(): jnp.dot(mine, col_scale.astype(jnp.bfloat16), preferred_element_type=jnp....  29.7 us
    reduce_sum x2, other arithmetic, unit_columns(): jnp.sum(values * values, axis=0, keepdims=True) + epsilon  9.15 us
  transfers between devices with their start and end apart: 2, of which 1 were waited for; matrix products, arithmetic and copies ran while one was open for 24% of the time, Pallas kernels for 0%

profile of v1, /device:TPU:0, one launch (start us, length us, event | category | flops | bytes accessed | tf_op | source)
XLA Modules:
  0.0 353.2 jit_solution(14631771199979908680)
XLA Ops:
  6.5 0.0 all-gather.5.cloned.1.call-start
  6.5 0.7 all-gather.5.cloned.1.call-update
  7.3 0.0 all-gather.3.cloned.1.call-start
  7.3 0.7 all-gather.3.cloned.1.call-update
  8.0 1.1 fusion.12
  9.1 2.0 fusion.4
  11.2 45.3 %all-gather.5.cloned.1.call-done = bf16[3072,256]{1,0:T(8,128)(2,1)} async-done(((bf16[384,256]{1,0:T(8,128)(2,1)}), bf16[3072,256]{1,0:T(8,128)(2,1)}) %all-gather.5.cloned.1.call-update) | async-done | bytes 1572880 | tf_op jit(solution)/shard_map/all_gather | solution.py:31
  56.4 1.9 fusion.6
  58.4 15.4 %exponential_convert_fusion = bf16[3072,4096]{1,0:T(8,128)(2,1)} fusion(bf16[256,4096]{1,0:T(8,128)(2,1)} %param.3, f32[4096]{0:T(1024)S(1)} %add_rsqrt_fusion.1, bf16[3072,256]{1,0:T(8,128)(2,1)} %all-gather.5.cloned.1.call-done, f32[3072]{0:T(1024)S(1)} %add_rsqrt_fusion.2), kind=kOutput, calls=%fused_computation.1 | convolution fusion | flops 6473121792 | bytes 28864512 | tf_op jit(solution)/shard_map/dot_general | solution.py:25
  73.7 0.0 copy-start
  73.7 11.5 %fusion.16 = f32[1,4096]{1,0:T(1,128)S(1)} fusion(bf16[3072,4096]{1,0:T(8,128)(2,1)} %exponential_convert_fusion), kind=kOutput, calls=%fused_computation.31 | convolution fusion | flops 25165824 | bytes 25182208 | tf_op jit(solution)/shard_map/dot_general | solution.py:34
  85.3 4.0 %copy-done = bf16[3072,4096]{1,0:T(8,128)(2,1)S(1)} copy-done((bf16[3072,4096]{1,0:T(8,128)(2,1)S(1)}, bf16[3072,4096]{1,0:T(8,128)(2,1)}, u32[]{:S(2)}) %copy-start) | copy-done | bytes 25165848
  89.3 6.6 %fusion.21 = f32[1,3072]{1,0:T(1,128)S(1)} fusion(bf16[3072,4096]{1,0:T(8,128)(2,1)S(1)} %copy-done, bf16[4096,1]{0,1:T(2,128)(2,1)S(1)} %reshape.28), kind=kOutput, calls=%fused_computation.38 | convolution fusion | flops 25165824 | bytes 25186304 | tf_op jit(solution)/shard_map/dot_general | solution.py:35
  95.8 43.7 %psum.21 = f32[3072]{0:T(1024)S(1)} all-reduce(f32[3072]{0:T(1024)S(1)} %bitcast.21), channel_id=1, replica_groups=mesh['replica'=4,'dp'=8] {'dp','replica'}, use_global_device_ids=true, to_apply=%region_4.0 | all-reduce | flops 3072 | bytes 24576 | tf_op jit(solution)/shard_map/psum | solution.py:36
  139.6 11.9 %fusion.22 = f32[1,4096]{1,0:T(1,128)S(1)} fusion(bf16[3072,1]{0,1:T(2,128)(2,1)S(1)} %reshape.30, bf16[3072,4096]{1,0:T(8,128)(2,1)} %exponential_convert_fusion), kind=kOutput, calls=%fused_computation.39 | convolution fusion | flops 25165824 | bytes 25188352 | tf_op jit(solution)/shard_map/dot_general | solution.py:34
  151.5 11.6 %fusion.23 = f32[1,3072]{1,0:T(1,128)S(1)} fusion(bf16[3072,4096]{1,0:T(8,128)(2,1)} %exponential_convert_fusion, bf16[4096,1]{0,1:T(2,128)(2,1)S(1)} %reshape.32), kind=kOutput, calls=%fused_computation.40 | convolution fusion | flops 25165824 | bytes 25186304 | tf_op jit(solution)/shard_map/dot_general | solution.py:35
  163.1 49.0 %psum.22 = f32[3072]{0:T(1024)S(1)} all-reduce(f32[3072]{0:T(1024)S(1)} %bitcast.22), channel_id=1, replica_groups=mesh['replica'=4,'dp'=8] {'dp','replica'}, use_global_device_ids=true, to_apply=%region_5.0 | all-reduce | flops 3072 | bytes 24576 | tf_op jit(solution)/shard_map/psum | solution.py:36
  212.1 10.1 %fusion.24 = f32[1,4096]{1,0:T(1,128)S(1)} fusion(bf16[3072,1]{0,1:T(2,128)(2,1)S(1)} %reshape.34, bf16[3072,4096]{1,0:T(8,128)(2,1)} %exponential_convert_fusion), kind=kOutput, calls=%fused_computation.41 | convolution fusion | flops 25165824 | bytes 25188352 | tf_op jit(solution)/shard_map/dot_general | solution.py:34
  222.2 0.0 copy-start.1
  222.2 11.6 %fusion.25 = f32[1,3072]{1,0:T(1,128)S(1)} fusion(bf16[3072,4096]{1,0:T(8,128)(2,1)} %exponential_convert_fusion, bf16[4096,1]{0,1:T(2,128)(2,1)S(1)} %reshape.36), kind=kOutput, calls=%fused_computation.42 | convolution fusion | flops 25165824 | bytes 25186304 | tf_op jit(solution)/shard_map/dot_general | solution.py:35
  233.8 47.7 %psum.23 = f32[3072]{0:T(1024)S(1)} all-reduce(f32[3072]{0:T(1024)S(1)} %bitcast.20), channel_id=1, replica_groups=mesh['replica'=4,'dp'=8] {'dp','replica'}, use_global_device_ids=true, to_apply=%region_6.0 | all-reduce | flops 3072 | bytes 24576 | tf_op jit(solution)/shard_map/psum | solution.py:36
  281.5 32.1 %all_gather.11 = f32[32768]{0:T(1024)S(1)} all-gather(f32[4096]{0:T(1024)S(1)} %get-tuple-element.6), channel_id=1, replica_groups=mesh['replica'=4,'dp'=8] {'dp'}, dimensions={0}, use_global_device_ids=true | all-gather | bytes 147456 | tf_op jit(solution)/shard_map/all_gather | solution.py:37
  313.6 0.1 fusion.18
  313.7 0.0 all-gather.3.cloned.1.call-done
  313.7 7.1 %fusion = f32[32768]{0:T(1024)S(1)} fusion(bf16[256,32768]{1,0:T(8,128)(2,1)} %all-gather.3.cloned.1.call-done), kind=kLoop, calls=%fused_computation.5 | loop fusion | flops 25133056 | bytes 16908288 | tf_op jit(solution)/shard_map/reduce_sum | solution.py:19
  320.8 0.0 copy-done.1
  320.9 25.5 %multiply_convert_fusion = bf16[384,32768]{1,0:T(8,128)(2,1)} fusion(f32[32768]{0:T(1024)S(1)} %all_gather.11, f32[384]{0:T(512)S(1)} %fusion.18, bf16[256,32768]{1,0:T(8,128)(2,1)} %all-gather.3.cloned.1.call-done, f32[32768]{0:T(1024)S(1)} %add_rsqrt_fusion, bf16[384,256]{1,0:T(8,128)(2,1)S(1)} %copy-done.1, f32[384]{0:T(512)S(1)} %add_rsqrt_fusion.3), kind=kOutput, calls=%fused_computation | convolution fusion | flops 6543409152 | bytes 42404864 | tf_op jit(solution)/shard_map/dot_general | solution.py:25
  (14 shorter events, 0.1 us)
Async XLA Ops:
  6.5 49.9 %all-gather.5.cloned.1.call-start = ((), (), s32[]{:S(2)}) async-start(), calls=%async_computation.1 | async-start | bytes 1769472 | tf_op jit(solution)/shard_map/all_gather | solution.py:31
  7.3 306.4 %all-gather.3.cloned.1.call-start = ((), (), s32[]{:S(2)}) async-start(), calls=%async_computation | async-start | bytes 18874368 | tf_op jit(solution)/shard_map/all_gather | solution.py:39
  73.7 15.5 %copy-start = (bf16[3072,4096]{1,0:T(8,128)(2,1)S(1)}, bf16[3072,4096]{1,0:T(8,128)(2,1)}, u32[]{:S(2)}) copy-start(bf16[3072,4096]{1,0:T(8,128)(2,1)} %exponential_convert_fusion) | copy-start | bytes 75497472
  222.2 98.6 %copy-start.1 = (bf16[384,256]{1,0:T(8,128)(2,1)S(1)}, bf16[384,256]{1,0:T(8,128)(2,1)}, u32[]{:S(2)}) copy-start(bf16[384,256]{1,0:T(8,128)(2,1)} %param.2) | copy-start | bytes 589828
Sparse Core Ops, SparseCore 0:
  9.5 46.8 all-gather.4
  58.6 229.0 all-gather.2
